TPU v7x, 128 devices: a whole 4x4x4 slice. The times are simulated.
128 devices in a mesh: dp: 16 (over z, x_lo, core), space: 8 (over x_hi, y).
Axes of the slice: x: 4 (x_hi: 2, x_lo: 2; x = x_hi * 2 + x_lo), y: 4, z: 4, core: 2. Of those that a mesh axis runs over, the one named last changes fastest.
Arguments:
- features: bfloat16 [16, 128, 64, 1024], P('dp', 'space'), may hold values from -6 to 6
- target: bfloat16 [16, 128, 64, 1024], P('dp', 'space'), may hold values from -6 to 6
- anchors: int32 [16, 2], P('dp'), may hold values from 0 to 64512
- w_first: bfloat16 [3, 3, 64, 64], replicated, may hold values from -0.25 to 0.25
- b_first: float32 [64], replicated, may hold values from -3 to 3
- w_second: bfloat16 [3, 3, 64, 64], replicated, may hold values from -0.25 to 0.25
- b_second: float32 [64], replicated, may hold values from -3 to 3
Outputs:
- back_input: bfloat16 [16, 128, 64, 1024], P('dp', 'space')
- grad_w1: float32 [3, 3, 64, 64], replicated
- grad_b1: float32 [64], replicated
- grad_w2: float32 [3, 3, 64, 64], replicated
- grad_b2: float32 [64], replicated
All inputs are finite; a program needn't handle non-finite values.
Results may differ from a plain program's by a relative error of at most 0.0075.
Values may be sent and summed in bfloat16 or wider, within the bound.
No kernel may reach another device: no remote copies, remote signals or barrier semaphores. Data moves between devices by JAX's collectives and lax.ppermute only.
A program may use at most 128 MiB of HBM per device.

v0:
```python
import math
import jax
import jax.numpy as jnp
from jax import lax
from jax.sharding import PartitionSpec as P


def extended(value, sides, width):
    for axis, dim in sides:
        size, length = (lax.axis_size(axis), value.shape[dim])
        up = [(i, (i + 1) % size) for i in range(size - 1)]
        down = [(j, i) for i, j in up]
        last = lax.slice_in_dim(value, length - width, length, axis=dim)
        first = lax.slice_in_dim(value, 0, width, axis=dim)
        before = lax.ppermute(last, axis, up)
        after = lax.ppermute(first, axis, down)
        value = jnp.concatenate([before, value, after], axis=dim)
    return value


def shift_cols(tensor, offset):
    if offset == 0:
        return tensor
    filler = jnp.zeros(tensor.shape[:-1] + (1,), tensor.dtype)
    if offset > 0:
        return jnp.concatenate([tensor[..., 1:], filler], axis=-1)
    return jnp.concatenate([filler, tensor[..., :-1]], axis=-1)


def unfold(padded):
    inner = padded.shape[1] - 2
    pieces = [
        shift_cols(padded[:, row_off : row_off + inner], col_off - 1)
        for row_off in range(3)
        for col_off in range(3)
    ]
    return jnp.concatenate(pieces, axis=2)


def unfold_back(padded):
    inner = padded.shape[1] - 2
    pieces = [
        shift_cols(padded[:, 2 - row_off : 2 - row_off + inner], 1 - col_off)
        for row_off in range(3)
        for col_off in range(3)
    ]
    return jnp.concatenate(pieces, axis=2)


def forward_matrix(kernel):
    return jnp.transpose(kernel, (2, 0, 1, 3)).reshape(kernel.shape[2], -1)


def backward_matrix(kernel):
    return jnp.transpose(kernel, (3, 0, 1, 2)).reshape(kernel.shape[3], -1)


def fold_kernel(matrix):
    channels = matrix.shape[0]
    return jnp.transpose(matrix.reshape(channels, 3, 3, -1), (1, 2, 0, 3))


def coords(anchor_rows, row_ids, columns, channels):
    chan_ids = jnp.arange(channels, dtype=jnp.int32)
    periods = 4 * jnp.left_shift(jnp.ones_like(chan_ids), chan_ids % 8)
    scaled = 2.0 * math.pi / periods.astype(jnp.float32)
    row_pos = anchor_rows[:, 0][:, None, None] + row_ids[None, :, None]
    row_wave = jnp.sin(
        (row_pos % periods[None, None, :]).astype(jnp.float32) * scaled[None, None, :]
    )
    col_ids = jnp.arange(columns, dtype=jnp.int32)
    col_pos = anchor_rows[:, 1][:, None, None] + col_ids[None, None, :]
    col_wave = jnp.sin(
        (col_pos % periods[None, :, None]).astype(jnp.float32) * scaled[None, :, None]
    )
    use_rows = (chan_ids < channels // 2)[None, None, :, None]
    return jnp.where(use_rows, row_wave[..., None], col_wave[:, None])


def gelu_grad(pre_act, upstream):
    return jax.vjp(lambda inputs: jax.nn.gelu(inputs, approximate=True), pre_act)[1](upstream)[0]


def mixing(form, left, right):
    return jnp.einsum(form, left, right, preferred_element_type=jnp.float32)


def combine(pairs):
    flat_grads = jnp.concatenate([piece.reshape(-1) for pair in pairs for piece in pair])
    total = lax.psum(flat_grads, ("dp", "space"))
    results = []
    start = 0
    for pair in pairs:
        for piece in pair:
            count = piece.size
            results.append(total[start : start + count].reshape(piece.shape))
            start = start + count
    return results


def shards(features, target, anchors, w_first, b_first, w_second, b_second):
    strip_rows = features.shape[1]
    columns = features.shape[3]
    channels = features.shape[2]
    dev_index = lax.axis_index("space")
    crop_rows = strip_rows * lax.axis_size("space")
    factor = 1.0 / math.sqrt(features.shape[0] * lax.axis_size("dp") * crop_rows * columns)
    row_ids = dev_index * strip_rows + jnp.arange(strip_rows, dtype=jnp.int32)
    geo = coords(anchors, row_ids, columns, channels)
    first = (features.astype(jnp.float32) + geo).astype(jnp.bfloat16)
    bias_one = b_first[None, None, :, None]
    first_pad = extended(first, (("space", 1),), 1)
    pre_act = mixing("dk,brkw->brdw", forward_matrix(w_first), unfold(first_pad)) + bias_one
    hidden = jax.nn.gelu(pre_act, approximate=True).astype(jnp.bfloat16)
    hidden_pad = extended(hidden, (("space", 1),), 1)
    output = (
        mixing("dk,brkw->brdw", forward_matrix(w_second), unfold(hidden_pad))
        + b_second[None, None, :, None]
    )
    misfit = (output - target.astype(jnp.float32)).astype(jnp.bfloat16)
    grad_w2 = fold_kernel(mixing("brdw,brkw->dk", misfit, unfold(hidden_pad))) * factor
    grad_b2 = jnp.sum(misfit.astype(jnp.float32), axis=(0, 1, 3)) * factor
    misfit_pad = extended(misfit, (("space", 1),), 1)
    back_hidden = mixing("ck,brkw->brcw", backward_matrix(w_second), unfold_back(misfit_pad))
    slope = gelu_grad(pre_act, back_hidden).astype(jnp.bfloat16)
    grad_w1 = fold_kernel(mixing("brdw,brkw->dk", slope, unfold(first_pad))) * factor
    grad_b1 = jnp.sum(slope.astype(jnp.float32), axis=(0, 1, 3)) * factor
    slope_pad = extended(slope, (("space", 1),), 1)
    back_input = mixing("ck,brkw->brcw", backward_matrix(w_first), unfold_back(slope_pad)).astype(
        jnp.bfloat16
    )
    grad_w2, grad_b2, grad_w1, grad_b1 = combine([(grad_w2, grad_b2), (grad_w1, grad_b1)])
    return (back_input, grad_w1, grad_b1, grad_w2, grad_b2)


def solution(mesh):
    in_specs = (
        P("dp", "space", None, None),
        P("dp", "space", None, None),
        P("dp", None),
        P(),
        P(),
        P(),
        P(),
    )
    out_specs = (P("dp", "space", None, None), P(), P(), P(), P())
    return jax.shard_map(shards, mesh=mesh, in_specs=in_specs, out_specs=out_specs, check_vma=False)
```

profile of v0, /device:TPU:1, one launch (start us, length us, event | category | flops | bytes accessed | tf_op | source)
XLA Modules:
  0.0 301.8 jit_solution(5083959459954517360)
XLA Ops:
  7.3 1.3 fusion.122
  8.6 0.6 iota_add_fusion
  9.2 0.7 add_add_fusion
  9.9 0.2 fusion.111
  10.2 3.5 %fusion.106 = f32[64,1024]{1,0:T(8,128)S(1)} fusion(f32[64]{0:T(128)S(1)} %convert_divide_fusion, s32[64]{0:T(128)S(1)} %compare_select_fusion, s32[1024]{0:T(1024)S(1)} %iota_add_fusion, pred[64]{0:T(512)(128)(4,1)S(1)} %broadcast_compare_fusion), kind=kLoop, calls=%fused_computation.138 | loop fusion | flops 589824 | bytes 266816 | tf_op jit(solution)/shard_map/sin | solution.py:73
  13.6 2.1 add_convert_fusion
  15.8 1.3 collective-permute-start.1
  17.1 4.8 %collective-permute-start = (bf16[1,1,64,1024]{3,2,1,0:T(8,128)(2,1)S(1)}, bf16[1,1,64,1024]{3,2,1,0:T(8,128)(2,1)S(1)}, u32[]{:S(2)}, u32[]{:S(2)}) collective-permute-start(bf16[1,1,64,1024]{3,2,1,0:T(8,128)(2,1)S(1)} %get-tuple-element.28), channel_id=1, source_target_pairs={{0,1},{1,2},{2,3},{3,4},{4,5},{5,6},{6,7},{8,9},{9,10},{10,11},{11... | collective-permute-start | bytes 393224 | tf_op jit(solution)/shard_map/ppermute | solution.py:15
  22.1 0.6 collective-permute-done.1
  22.7 1.0 collective-permute-done
  23.7 1.0 fusion.58
  24.7 0.9 pad_dynamic-update-slice_fusion.15
  25.6 0.2 fusion.60
  25.9 1.1 fusion.63
  27.0 1.2 pad_dynamic-update-slice_fusion.14
  28.2 0.6 constant_dynamic-update-slice_fusion
  28.7 0.3 pad_dynamic-update-slice_fusion.13
  29.1 1.2 pad_dynamic-update-slice_fusion.12
  30.5 1.1 fusion.65
  31.6 8.4 %fusion.35 = (bf16[1,16,64,1024]{3,2,1,0:T(8,128)(2,1)S(1)}, f32[16,1024,64]{1,2,0:T(8,128)}) fusion(f32[64]{0:T(128)S(1)} %copy-done.6, bf16[64,576,1]{0,1,2:T(8,128)(2,1)S(1)} %bitcast.173, bf16[1,16,576,1024]{3,2,1,0:T(8,128)(2,1)S(1)} %fusion.65), kind=kOutput, calls=%fused_computation.44 | convolution fusion | flops 1218445312 | bytes 25239808 | tf_op jit(solution)/shard_map/dk,brkw->brdw/dot_general | solution.py:85
  40.0 1.3 collective-permute-start.3
  41.3 4.6 %collective-permute-start.2 = (bf16[1,1,64,1024]{3,2,1,0:T(8,128)(2,1)S(1)}, bf16[1,1,64,1024]{3,2,1,0:T(8,128)(2,1)S(1)}, u32[]{:S(2)}, u32[]{:S(2)}) collective-permute-start(bf16[1,1,64,1024]{3,2,1,0:T(8,128)(2,1)S(1)} %get-tuple-element.22), channel_id=1, source_target_pairs={{0,1},{1,2},{2,3},{3,4},{4,5},{5,6},{6,7},{8,9},{9,10},{10,11},{11... | collective-permute-start | bytes 393224 | tf_op jit(solution)/shard_map/ppermute | solution.py:15
  46.1 1.5 collective-permute-done.2
  47.7 1.0 fusion.52
  48.7 0.9 pad_dynamic-update-slice_fusion.11
  49.8 1.1 fusion.67
  50.9 1.2 pad_dynamic-update-slice_fusion.10
  52.3 0.3 pad_dynamic-update-slice_fusion.9
  52.6 1.2 pad_dynamic-update-slice_fusion.8
  54.0 1.1 fusion.69
  55.1 8.4 %convert_reduce_fusion.1 = (f32[64]{0:T(128)S(1)}, bf16[1,16,64,1024]{3,2,1,0:T(8,128)(2,1)S(1)}) fusion(bf16[1,16,64,1024]{3,2,1,0:T(8,128)(2,1)} %param.8, f32[64]{0:T(128)S(1)} %copy-done.5, bf16[64,576,1]{0,1,2:T(8,128)(2,1)S(1)} %bitcast.167, bf16[1,16,576,1024]{3,2,1,0:T(8,128)(2,1)S(1)} %fusion.69), kind=kOutput, calls=%fused_computation.47 | convolution fusion | flops 1214251008 | bytes 23142912 | tf_op jit(solution)/shard_map/dk,brkw->brdw/dot_general | solution.py:85
  63.5 12.3 %fusion.92 = f32[3,3,64,64]{3,2,1,0:T(8,128)S(1)} fusion(bf16[3,3,64,16,1024]{4,2,1,0,3:T(8,128)(2,1)} %bitcast.166, bf16[1,16,64,1024]{3,2,1,0:T(8,128)(2,1)S(1)} %get-tuple-element.38), kind=kOutput, calls=%fused_computation.128 | convolution fusion | flops 1207996416 | bytes 21118976 | tf_op jit(solution)/shard_map/brdw,brkw->dk/dot_general | solution.py:85
  76.0 4.1 %collective-permute-start.5 = (bf16[1,1,64,1024]{3,2,1,0:T(8,128)(2,1)S(1)}, bf16[1,1,64,1024]{3,2,1,0:T(8,128)(2,1)S(1)}, u32[]{:S(2)}, u32[]{:S(2)}) collective-permute-start(bf16[1,1,64,1024]{3,2,1,0:T(8,128)(2,1)S(1)} %get-tuple-element.15), channel_id=1, source_target_pairs={{0,1},{1,2},{2,3},{3,4},{4,5},{5,6},{6,7},{8,9},{9,10},{10,11},{11... | collective-permute-start | bytes 393224 | tf_op jit(solution)/shard_map/ppermute | solution.py:15
  80.0 1.7 collective-permute-start.4
  82.0 5.7 %collective-permute-done.4 = bf16[1,1,64,1024]{3,2,1,0:T(8,128)(2,1)S(1)} collective-permute-done((bf16[1,1,64,1024]{3,2,1,0:T(8,128)(2,1)S(1)}, bf16[1,1,64,1024]{3,2,1,0:T(8,128)(2,1)S(1)}, u32[]{:S(2)}, u32[]{:S(2)}) %collective-permute-start.4) | collective-permute-done | bytes 131104 | tf_op jit(solution)/shard_map/ppermute | solution.py:16
  87.6 2.4 fusion.46
  90.0 0.3 pad_dynamic-update-slice_fusion.7
  90.4 0.2 fusion.48
  90.6 1.3 fusion.71
  91.9 0.3 pad_dynamic-update-slice_fusion.6
  92.5 1.2 pad_dynamic-update-slice_fusion.5
  93.6 0.3 pad_dynamic-update-slice_fusion.4
  94.0 0.2 fusion.45
  94.2 1.3 fusion.73
  95.5 10.1 %convert_reduce_fusion = (f32[64]{0:T(128)S(1)}, bf16[1,16,64,1024]{3,2,1,0:T(8,128)(2,1)S(1)}) fusion(f32[64]{0:T(128)S(1)} %copy-done.6, f32[16,1024,64]{1,2,0:T(8,128)} %get-tuple-element.36, bf16[64,576,1]{0,1,2:T(8,128)(2,1)S(1)} %bitcast.172, bf16[1,16,576,1024]{3,2,1,0:T(8,128)(2,1)S(1)} %fusion.73), kind=kOutput, calls=%fused_computation.46 | convolution fusion | flops 1232076800 | bytes 25240064 | tf_op jit(solution)/shard_map/ck,brkw->brcw/dot_general | solution.py:85
  105.6 12.5 %fusion.101 = f32[3,3,64,64]{3,2,1,0:T(8,128)S(1)} fusion(bf16[3,3,64,16,1024]{4,2,1,0,3:T(8,128)(2,1)} %bitcast.170, bf16[1,16,64,1024]{3,2,1,0:T(8,128)(2,1)S(1)} %get-tuple-element.40), kind=kOutput, calls=%fused_computation.131 | convolution fusion | flops 1207996416 | bytes 21118976 | tf_op jit(solution)/shard_map/brdw,brkw->dk/dot_general | solution.py:85
  118.3 7.4 %collective-permute-start.7 = (bf16[1,1,64,1024]{3,2,1,0:T(8,128)(2,1)S(1)}, bf16[1,1,64,1024]{3,2,1,0:T(8,128)(2,1)S(1)}, u32[]{:S(2)}, u32[]{:S(2)}) collective-permute-start(bf16[1,1,64,1024]{3,2,1,0:T(8,128)(2,1)S(1)} %get-tuple-element.9), channel_id=1, source_target_pairs={{0,1},{1,2},{2,3},{3,4},{4,5},{5,6},{6,7},{8,9},{9,10},{10,11},{11... | collective-permute-start | bytes 393224 | tf_op jit(solution)/shard_map/ppermute | solution.py:15
  125.7 1.3 collective-permute-start.6
  127.0 4.3 %concatenate.165 = f32[73856]{0:T(1024)} concatenate(f32[36864]{0:T(1024)S(1)} %reshape.374, f32[64]{0:T(128)S(1)} %broadcast_multiply_fusion.1, f32[36864]{0:T(1024)S(1)} %reshape.376, f32[64]{0:T(128)S(1)} %broadcast_multiply_fusion), dimensions={0} | concatenate | bytes 590848 | tf_op jit(solution)/shard_map/concatenate | solution.py:89
  131.3 4.1 %collective-permute-done.6 = bf16[1,1,64,1024]{3,2,1,0:T(8,128)(2,1)S(1)} collective-permute-done((bf16[1,1,64,1024]{3,2,1,0:T(8,128)(2,1)S(1)}, bf16[1,1,64,1024]{3,2,1,0:T(8,128)(2,1)S(1)}, u32[]{:S(2)}, u32[]{:S(2)}) %collective-permute-start.6) | collective-permute-done | bytes 131104 | tf_op jit(solution)/shard_map/ppermute | solution.py:16
  135.4 2.4 fusion.40
  137.8 0.3 pad_dynamic-update-slice_fusion.3
  138.1 0.2 fusion.42
  138.4 1.3 fusion.75
  139.6 0.3 pad_dynamic-update-slice_fusion.2
  140.2 1.2 pad_dynamic-update-slice_fusion.1
  141.4 0.3 pad_dynamic-update-slice_fusion
  141.9 1.3 fusion.77
  143.2 6.7 %convert_bitcast_fusion = bf16[1,16,64,1024]{3,2,1,0:T(8,128)(2,1)} fusion(bf16[64,576,1]{0,1,2:T(8,128)(2,1)S(1)} %bitcast.169, bf16[1,16,576,1024]{3,2,1,0:T(8,128)(2,1)S(1)} %fusion.77), kind=kOutput, calls=%fused_computation.109 | convolution fusion | flops 1209008128 | bytes 21045248 | tf_op jit(solution)/shard_map/ck,brkw->brcw/dot_general | solution.py:85
  150.0 140.8 %all-reduce.26.cloned.1.call-done = f32[73856]{0:T(1024)} async-done(((f32[73856]{0:T(1024)}), f32[73856]{0:T(1024)}) %all-reduce.26.cloned.1.call-update) | async-done | bytes 295440 | tf_op jit(solution)/shard_map/psum | solution.py:90
  290.8 1.1 fusion.121
  291.9 0.8 reshape.378
  292.7 0.8 reshape.377
  293.5 1.3 fusion.120
  (40 shorter events, 2.5 us)
Async XLA Ops:
  7.2 14.8 %copy-start.2 = (bf16[3,3,64,64]{3,2,1,0:T(8,128)(2,1)S(1)}, bf16[3,3,64,64]{3,2,1,0:T(8,128)(2,1)}, u32[]{:S(2)}) copy-start(bf16[3,3,64,64]{3,2,1,0:T(8,128)(2,1)} %param.10) | copy-start | bytes 221188
  7.2 283.6 %all-reduce.26.cloned.1.call-start = ((), (), s32[]{:S(2)}) async-start(), calls=%async_computation | async-start | bytes 598016 | tf_op jit(solution)/shard_map/psum | solution.py:90
  15.8 6.9 %collective-permute-start.1 = (bf16[1,1,64,1024]{3,2,1,0:T(8,128)(2,1)S(1)}, bf16[1,1,64,1024]{3,2,1,0:T(8,128)(2,1)S(1)}, u32[]{:S(2)}, u32[]{:S(2)}) collective-permute-start(bf16[1,1,64,1024]{3,2,1,0:T(8,128)(2,1)S(1)} %get-tuple-element.27), channel_id=1, source_target_pairs={{1,0},{2,1},{3,2},{4,3},{5,4},{6,5},{7,6},{9,8},{10,9},{11,10},{12... | collective-permute-start | bytes 393224 | tf_op jit(solution)/shard_map/ppermute | solution.py:16
  17.1 6.6 %collective-permute-start = (bf16[1,1,64,1024]{3,2,1,0:T(8,128)(2,1)S(1)}, bf16[1,1,64,1024]{3,2,1,0:T(8,128)(2,1)S(1)}, u32[]{:S(2)}, u32[]{:S(2)}) collective-permute-start(bf16[1,1,64,1024]{3,2,1,0:T(8,128)(2,1)S(1)} %get-tuple-element.28), channel_id=1, source_target_pairs={{0,1},{1,2},{2,3},{3,4},{4,5},{5,6},{6,7},{8,9},{9,10},{10,11},{11... | collective-permute-start | bytes 393224 | tf_op jit(solution)/shard_map/ppermute | solution.py:15
  25.9 2.3 copy-start.1
  30.2 1.4 copy-start.6
  31.6 8.4 %copy-start.3 = (bf16[1,16,576,1024]{3,2,1,0:T(8,128)(2,1)}, bf16[1,16,576,1024]{3,2,1,0:T(8,128)(2,1)S(1)}, u32[]{:S(2)}) copy-start(bf16[1,16,576,1024]{3,2,1,0:T(8,128)(2,1)S(1)} %fusion.65) | copy-start | bytes 56623108
  31.6 14.3 %copy-start.4 = (bf16[3,3,64,64]{3,2,1,0:T(8,128)(2,1)S(1)}, bf16[3,3,64,64]{3,2,1,0:T(8,128)(2,1)}, u32[]{:S(2)}) copy-start(bf16[3,3,64,64]{3,2,1,0:T(8,128)(2,1)} %param.12) | copy-start | bytes 221188
  40.0 6.1 %collective-permute-start.3 = (bf16[1,1,64,1024]{3,2,1,0:T(8,128)(2,1)S(1)}, bf16[1,1,64,1024]{3,2,1,0:T(8,128)(2,1)S(1)}, u32[]{:S(2)}, u32[]{:S(2)}) collective-permute-start(bf16[1,1,64,1024]{3,2,1,0:T(8,128)(2,1)S(1)} %get-tuple-element.21), channel_id=1, source_target_pairs={{1,0},{2,1},{3,2},{4,3},{5,4},{6,5},{7,6},{9,8},{10,9},{11,10},{12... | collective-permute-start | bytes 393224 | tf_op jit(solution)/shard_map/ppermute | solution.py:16
  41.3 6.3 %collective-permute-start.2 = (bf16[1,1,64,1024]{3,2,1,0:T(8,128)(2,1)S(1)}, bf16[1,1,64,1024]{3,2,1,0:T(8,128)(2,1)S(1)}, u32[]{:S(2)}, u32[]{:S(2)}) collective-permute-start(bf16[1,1,64,1024]{3,2,1,0:T(8,128)(2,1)S(1)} %get-tuple-element.22), channel_id=1, source_target_pairs={{0,1},{1,2},{2,3},{3,4},{4,5},{5,6},{6,7},{8,9},{9,10},{10,11},{11... | collective-permute-start | bytes 393224 | tf_op jit(solution)/shard_map/ppermute | solution.py:15
  53.8 1.3 copy-start.5
  55.1 8.4 %copy-start = (bf16[1,16,576,1024]{3,2,1,0:T(8,128)(2,1)}, bf16[1,16,576,1024]{3,2,1,0:T(8,128)(2,1)S(1)}, u32[]{:S(2)}) copy-start(bf16[1,16,576,1024]{3,2,1,0:T(8,128)(2,1)S(1)} %fusion.69) | copy-start | bytes 56623108
  76.0 6.0 %collective-permute-start.5 = (bf16[1,1,64,1024]{3,2,1,0:T(8,128)(2,1)S(1)}, bf16[1,1,64,1024]{3,2,1,0:T(8,128)(2,1)S(1)}, u32[]{:S(2)}, u32[]{:S(2)}) collective-permute-start(bf16[1,1,64,1024]{3,2,1,0:T(8,128)(2,1)S(1)} %get-tuple-element.15), channel_id=1, source_target_pairs={{0,1},{1,2},{2,3},{3,4},{4,5},{5,6},{6,7},{8,9},{9,10},{10,11},{11... | collective-permute-start | bytes 393224 | tf_op jit(solution)/shard_map/ppermute | solution.py:15
  80.0 7.6 %collective-permute-start.4 = (bf16[1,1,64,1024]{3,2,1,0:T(8,128)(2,1)S(1)}, bf16[1,1,64,1024]{3,2,1,0:T(8,128)(2,1)S(1)}, u32[]{:S(2)}, u32[]{:S(2)}) collective-permute-start(bf16[1,1,64,1024]{3,2,1,0:T(8,128)(2,1)S(1)} %get-tuple-element.16), channel_id=1, source_target_pairs={{1,0},{2,1},{3,2},{4,3},{5,4},{6,5},{7,6},{9,8},{10,9},{11,10},{12... | collective-permute-start | bytes 393224 | tf_op jit(solution)/shard_map/ppermute | solution.py:16
  118.3 13.1 %collective-permute-start.7 = (bf16[1,1,64,1024]{3,2,1,0:T(8,128)(2,1)S(1)}, bf16[1,1,64,1024]{3,2,1,0:T(8,128)(2,1)S(1)}, u32[]{:S(2)}, u32[]{:S(2)}) collective-permute-start(bf16[1,1,64,1024]{3,2,1,0:T(8,128)(2,1)S(1)} %get-tuple-element.9), channel_id=1, source_target_pairs={{0,1},{1,2},{2,3},{3,4},{4,5},{5,6},{6,7},{8,9},{9,10},{10,11},{11... | collective-permute-start | bytes 393224 | tf_op jit(solution)/shard_map/ppermute | solution.py:15
  125.7 9.7 %collective-permute-start.6 = (bf16[1,1,64,1024]{3,2,1,0:T(8,128)(2,1)S(1)}, bf16[1,1,64,1024]{3,2,1,0:T(8,128)(2,1)S(1)}, u32[]{:S(2)}, u32[]{:S(2)}) collective-permute-start(bf16[1,1,64,1024]{3,2,1,0:T(8,128)(2,1)S(1)} %get-tuple-element.10), channel_id=1, source_target_pairs={{1,0},{2,1},{3,2},{4,3},{5,4},{6,5},{7,6},{9,8},{10,9},{11,10},{12... | collective-permute-start | bytes 393224 | tf_op jit(solution)/shard_map/ppermute | solution.py:16
Sparse Core Ops, SparseCore 0:
  131.4 159.3 all-reduce.25
where the time goes:
time: 306 us; the launch traced here: 302 us
  waiting for transfers between devices  154 us (50%)
  matrix products  58.4 us (19%)
  starting transfers between devices  26.5 us (9%)
  other arithmetic  25.8 us (8%)
  local copies, waits for them, and re-layouts  22.4 us (7%)
  between operations  14.9 us (5%)
    psum x1, waiting for transfers between devices, combine(): total = lax.psum(flat_grads, ('dp', 'space'))  141 us
    dot_general x6, matrix products, mixing(): return jnp.einsum(form, left, right, preferred_element_type=jnp.float32)  58.4 us
    ppermute x4, starting transfers between devices, extended(): before = lax.ppermute(last, axis, up)  20.9 us
    unnamed x33, local copies, waits for them, and re-layouts  12.2 us
    ppermute x4, waiting for transfers between devices, extended(): after = lax.ppermute(first, axis, down)  10.4 us
    unnamed x13, other arithmetic  7.09 us
    concatenate x4, other arithmetic, extended(): value = jnp.concatenate([before, value, after], axis=dim)  6.78 us
  transfers between devices with their start and end apart: 9, of which 7 were waited for; matrix products, arithmetic and copies ran while one was open for 6% of the time, Pallas kernels for 0%

commit v1 on v0

--- a/solution.py
+++ b/solution.py
@@ -87,7 +87,7 @@
 
 def combine(pairs):
     flat_grads = jnp.concatenate([piece.reshape(-1) for pair in pairs for piece in pair])
-    total = lax.psum(flat_grads, ("dp", "space"))
+    total = jnp.sum(lax.all_gather(flat_grads, ("dp", "space")), axis=0)
     results = []
     start = 0
     for pair in pairs:

time: 306 us -> 535 us (1.75)
  waiting for transfers between devices: 154 us -> 351 us
  other arithmetic: 25.8 us -> 61.4 us
    all_gather x0 -> x1, waiting for transfers between devices: none -> 334 us  [combine(): total = jnp.sum(lax.all_gather(flat_grads, ('dp', 'space')), axis=0)]
    psum x1 -> x0, waiting for transfers between devices: 141 us -> none  [combine(): total = lax.psum(flat_grads, ('dp', 'space'))]
    reduce_sum x0 -> x1, other arithmetic: none -> 35.6 us  [combine(): total = jnp.sum(lax.all_gather(flat_grads, ('dp', 'space')), axis=0)]
    unnamed x33 -> x34, local copies, waits for them, and re-layouts: 12.2 us -> 13 us
  transfers between devices with their start and end apart: 9 -> 9, of which waited for: 7 -> 8; matrix products, arithmetic and copies ran while one was open for 6% -> 3% of each run, Pallas kernels for 0% -> 0%
where the time goes in v1:
time: 535 us; the launch traced here: 531 us
  waiting for transfers between devices  351 us (66%)
  other arithmetic  61.4 us (11%)
  matrix products  58.4 us (11%)
  starting transfers between devices  26.5 us (5%)
  local copies, waits for them, and re-layouts  18.8 us (4%)
  between operations  14.9 us (3%)
    all_gather x1, waiting for transfers between devices, combine(): total = jnp.sum(lax.all_gather(flat_grads, ('dp', 'space')), axis=0)  334 us
    dot_general x6, matrix products, mixing(): return jnp.einsum(form, left, right, preferred_element_type=jnp.float32)  58.4 us
    reduce_sum x1, other arithmetic, combine(): total = jnp.sum(lax.all_gather(flat_grads, ('dp', 'space')), axis=0)  35.6 us
    ppermute x4, starting transfers between devices, extended(): before = lax.ppermute(last, axis, up)  20.9 us
    ppermute x4, waiting for transfers between devices, extended(): after = lax.ppermute(first, axis, down)  14.1 us
    unnamed x34, local copies, waits for them, and re-layouts  13 us
  transfers between devices with their start and end apart: 9, of which 8 were waited for; matrix products, arithmetic and copies ran while one was open for 3% of the time, Pallas kernels for 0%

profile of v1, /device:TPU:1, one launch (start us, length us, event | category | flops | bytes accessed | tf_op | source)
XLA Modules:
  0.0 531.0 jit_solution(13210614910652338709)
XLA Ops:
  7.3 1.3 fusion.122
  8.6 0.6 iota_add_fusion
  9.2 0.7 add_add_fusion
  9.9 0.2 fusion.111
  10.2 3.5 fusion.106
  13.6 2.1 add_convert_fusion
  15.8 1.3 collective-permute-start.1
  17.1 4.8 collective-permute-start
  22.1 0.6 collective-permute-done.1
  22.7 1.0 collective-permute-done
  23.7 1.0 fusion.58
  24.7 0.9 pad_dynamic-update-slice_fusion.15
  25.9 1.1 fusion.63
  27.0 1.2 pad_dynamic-update-slice_fusion.14
  28.2 0.6 constant_dynamic-update-slice_fusion
  28.7 0.3 pad_dynamic-update-slice_fusion.13
  29.1 1.2 pad_dynamic-update-slice_fusion.12
  30.5 1.1 fusion.65
  31.6 8.4 %fusion.35 = (bf16[1,16,64,1024]{3,2,1,0:T(8,128)(2,1)S(1)}, f32[16,1024,64]{1,2,0:T(8,128)}) fusion(f32[64]{0:T(128)S(1)} %copy-done.6, bf16[64,576,1]{0,1,2:T(8,128)(2,1)S(1)} %bitcast.173, bf16[1,16,576,1024]{3,2,1,0:T(8,128)(2,1)S(1)} %fusion.65), kind=kOutput, calls=%fused_computation.44 | convolution fusion | flops 1218445312 | bytes 25239808 | tf_op jit(solution)/shard_map/dk,brkw->brdw/dot_general | solution.py:85
  40.0 1.3 collective-permute-start.3
  41.3 4.6 collective-permute-start.2
  46.1 1.5 collective-permute-done.2
  47.7 1.0 fusion.52
  48.7 0.9 pad_dynamic-update-slice_fusion.11
  49.8 1.1 fusion.67
  50.9 1.2 pad_dynamic-update-slice_fusion.10
  52.3 0.3 pad_dynamic-update-slice_fusion.9
  52.6 1.2 pad_dynamic-update-slice_fusion.8
  54.0 1.1 fusion.69
  55.1 8.4 %convert_reduce_fusion.1 = (f32[64]{0:T(128)S(1)}, bf16[1,16,64,1024]{3,2,1,0:T(8,128)(2,1)S(1)}) fusion(bf16[1,16,64,1024]{3,2,1,0:T(8,128)(2,1)} %param.8, f32[64]{0:T(128)S(1)} %copy-done.5, bf16[64,576,1]{0,1,2:T(8,128)(2,1)S(1)} %bitcast.167, bf16[1,16,576,1024]{3,2,1,0:T(8,128)(2,1)S(1)} %fusion.69), kind=kOutput, calls=%fused_computation.47 | convolution fusion | flops 1214251008 | bytes 23142912 | tf_op jit(solution)/shard_map/dk,brkw->brdw/dot_general | solution.py:85
  63.5 12.3 %fusion.92 = f32[3,3,64,64]{3,2,1,0:T(8,128)S(1)} fusion(bf16[3,3,64,16,1024]{4,2,1,0,3:T(8,128)(2,1)} %bitcast.166, bf16[1,16,64,1024]{3,2,1,0:T(8,128)(2,1)S(1)} %get-tuple-element.38), kind=kOutput, calls=%fused_computation.128 | convolution fusion | flops 1207996416 | bytes 21118976 | tf_op jit(solution)/shard_map/brdw,brkw->dk/dot_general | solution.py:85
  76.0 4.1 collective-permute-start.5
  80.0 1.7 collective-permute-start.4
  82.0 5.7 %collective-permute-done.4 = bf16[1,1,64,1024]{3,2,1,0:T(8,128)(2,1)S(1)} collective-permute-done((bf16[1,1,64,1024]{3,2,1,0:T(8,128)(2,1)S(1)}, bf16[1,1,64,1024]{3,2,1,0:T(8,128)(2,1)S(1)}, u32[]{:S(2)}, u32[]{:S(2)}) %collective-permute-start.4) | collective-permute-done | bytes 131104 | tf_op jit(solution)/shard_map/ppermute | solution.py:16
  87.6 2.4 fusion.46
  90.0 0.3 pad_dynamic-update-slice_fusion.7
  90.4 0.2 fusion.48
  90.6 1.3 fusion.71
  91.9 0.3 pad_dynamic-update-slice_fusion.6
  92.5 1.2 pad_dynamic-update-slice_fusion.5
  93.6 0.3 pad_dynamic-update-slice_fusion.4
  94.2 1.3 fusion.73
  95.5 10.1 %convert_reduce_fusion = (f32[64]{0:T(128)S(1)}, bf16[1,16,64,1024]{3,2,1,0:T(8,128)(2,1)S(1)}) fusion(f32[64]{0:T(128)S(1)} %copy-done.6, f32[16,1024,64]{1,2,0:T(8,128)} %get-tuple-element.36, bf16[64,576,1]{0,1,2:T(8,128)(2,1)S(1)} %bitcast.172, bf16[1,16,576,1024]{3,2,1,0:T(8,128)(2,1)S(1)} %fusion.73), kind=kOutput, calls=%fused_computation.46 | convolution fusion | flops 1232076800 | bytes 25240064 | tf_op jit(solution)/shard_map/ck,brkw->brcw/dot_general | solution.py:85
  105.6 12.5 %fusion.101 = f32[3,3,64,64]{3,2,1,0:T(8,128)S(1)} fusion(bf16[3,3,64,16,1024]{4,2,1,0,3:T(8,128)(2,1)} %bitcast.170, bf16[1,16,64,1024]{3,2,1,0:T(8,128)(2,1)S(1)} %get-tuple-element.40), kind=kOutput, calls=%fused_computation.131 | convolution fusion | flops 1207996416 | bytes 21118976 | tf_op jit(solution)/shard_map/brdw,brkw->dk/dot_general | solution.py:85
  118.2 1.6 concatenate.165
  119.8 0.9 reshape.380
  120.8 7.4 %collective-permute-start.7 = (bf16[1,1,64,1024]{3,2,1,0:T(8,128)(2,1)S(1)}, bf16[1,1,64,1024]{3,2,1,0:T(8,128)(2,1)S(1)}, u32[]{:S(2)}, u32[]{:S(2)}) collective-permute-start(bf16[1,1,64,1024]{3,2,1,0:T(8,128)(2,1)S(1)} %get-tuple-element.9), channel_id=1, source_target_pairs={{0,1},{1,2},{2,3},{3,4},{4,5},{5,6},{6,7},{8,9},{9,10},{10,11},{11... | collective-permute-start | bytes 393224 | tf_op jit(solution)/shard_map/ppermute | solution.py:15
  128.2 1.3 collective-permute-start.6
  129.5 0.6 collective-permute-done.7
  130.1 7.8 %collective-permute-done.6 = bf16[1,1,64,1024]{3,2,1,0:T(8,128)(2,1)S(1)} collective-permute-done((bf16[1,1,64,1024]{3,2,1,0:T(8,128)(2,1)S(1)}, bf16[1,1,64,1024]{3,2,1,0:T(8,128)(2,1)S(1)}, u32[]{:S(2)}, u32[]{:S(2)}) %collective-permute-start.6) | collective-permute-done | bytes 131104 | tf_op jit(solution)/shard_map/ppermute | solution.py:16
  137.9 2.4 fusion.40
  140.3 0.3 pad_dynamic-update-slice_fusion.3
  140.6 0.2 fusion.42
  140.9 1.3 fusion.75
  142.1 0.3 pad_dynamic-update-slice_fusion.2
  142.7 1.2 pad_dynamic-update-slice_fusion.1
  143.9 0.3 pad_dynamic-update-slice_fusion
  144.4 1.3 fusion.77
  145.7 6.7 %convert_bitcast_fusion = bf16[1,16,64,1024]{3,2,1,0:T(8,128)(2,1)} fusion(bf16[64,576,1]{0,1,2:T(8,128)(2,1)S(1)} %bitcast.169, bf16[1,16,576,1024]{3,2,1,0:T(8,128)(2,1)S(1)} %fusion.77), kind=kOutput, calls=%fused_computation.109 | convolution fusion | flops 1209008128 | bytes 21045248 | tf_op jit(solution)/shard_map/ck,brkw->brcw/dot_general | solution.py:85
  152.5 333.6 %all-gather.4.cloned.1.call-done = f32[128,1,73856]{2,1,0:T(1,128)} async-done(((f32[1,1,73856]{2,1,0:T(1,128)}), f32[128,1,73856]{2,1,0:T(1,128)}) %all-gather.4.cloned.1.call-update) | async-done | bytes 37814288 | tf_op jit(solution)/shard_map/all_gather | solution.py:90
  486.0 35.6 %reduce_sum.29 = f32[73856]{0:T(1024)S(1)} reduce(f32[128,1,73856]{2,1,0:T(1,128)} %all-gather.4.cloned.1.call-done, f32[]{:T(128)} %constant.63.clone.1), dimensions={0,1}, to_apply=%region_2.3 | reduce | flops 9379712 | bytes 38109700 | tf_op jit(solution)/shard_map/reduce_sum | solution.py:90
  521.7 0.6 fusion.120
  522.4 0.8 reshape.378
  523.2 0.8 reshape.377
  (42 shorter events, 3.1 us)
Async XLA Ops:
  7.2 14.8 %copy-start.2 = (bf16[3,3,64,64]{3,2,1,0:T(8,128)(2,1)S(1)}, bf16[3,3,64,64]{3,2,1,0:T(8,128)(2,1)}, u32[]{:S(2)}) copy-start(bf16[3,3,64,64]{3,2,1,0:T(8,128)(2,1)} %param.10) | copy-start | bytes 221188
  7.2 478.9 %all-gather.4.cloned.1.call-start = ((), (), s32[]{:S(2)}) async-start(), calls=%async_computation | async-start | bytes 38109696 | tf_op jit(solution)/shard_map/all_gather | solution.py:90
  15.8 6.9 %collective-permute-start.1 = (bf16[1,1,64,1024]{3,2,1,0:T(8,128)(2,1)S(1)}, bf16[1,1,64,1024]{3,2,1,0:T(8,128)(2,1)S(1)}, u32[]{:S(2)}, u32[]{:S(2)}) collective-permute-start(bf16[1,1,64,1024]{3,2,1,0:T(8,128)(2,1)S(1)} %get-tuple-element.27), channel_id=1, source_target_pairs={{1,0},{2,1},{3,2},{4,3},{5,4},{6,5},{7,6},{9,8},{10,9},{11,10},{12... | collective-permute-start | bytes 393224 | tf_op jit(solution)/shard_map/ppermute | solution.py:16
  17.1 6.6 %collective-permute-start = (bf16[1,1,64,1024]{3,2,1,0:T(8,128)(2,1)S(1)}, bf16[1,1,64,1024]{3,2,1,0:T(8,128)(2,1)S(1)}, u32[]{:S(2)}, u32[]{:S(2)}) collective-permute-start(bf16[1,1,64,1024]{3,2,1,0:T(8,128)(2,1)S(1)} %get-tuple-element.28), channel_id=1, source_target_pairs={{0,1},{1,2},{2,3},{3,4},{4,5},{5,6},{6,7},{8,9},{9,10},{10,11},{11... | collective-permute-start | bytes 393224 | tf_op jit(solution)/shard_map/ppermute | solution.py:15
  25.9 2.3 copy-start.1
  30.2 1.4 copy-start.6
  31.6 8.4 %copy-start.3 = (bf16[1,16,576,1024]{3,2,1,0:T(8,128)(2,1)}, bf16[1,16,576,1024]{3,2,1,0:T(8,128)(2,1)S(1)}, u32[]{:S(2)}) copy-start(bf16[1,16,576,1024]{3,2,1,0:T(8,128)(2,1)S(1)} %fusion.65) | copy-start | bytes 56623108
  31.6 14.3 %copy-start.4 = (bf16[3,3,64,64]{3,2,1,0:T(8,128)(2,1)S(1)}, bf16[3,3,64,64]{3,2,1,0:T(8,128)(2,1)}, u32[]{:S(2)}) copy-start(bf16[3,3,64,64]{3,2,1,0:T(8,128)(2,1)} %param.12) | copy-start | bytes 221188
  40.0 6.1 %collective-permute-start.3 = (bf16[1,1,64,1024]{3,2,1,0:T(8,128)(2,1)S(1)}, bf16[1,1,64,1024]{3,2,1,0:T(8,128)(2,1)S(1)}, u32[]{:S(2)}, u32[]{:S(2)}) collective-permute-start(bf16[1,1,64,1024]{3,2,1,0:T(8,128)(2,1)S(1)} %get-tuple-element.21), channel_id=1, source_target_pairs={{1,0},{2,1},{3,2},{4,3},{5,4},{6,5},{7,6},{9,8},{10,9},{11,10},{12... | collective-permute-start | bytes 393224 | tf_op jit(solution)/shard_map/ppermute | solution.py:16
  41.3 6.3 %collective-permute-start.2 = (bf16[1,1,64,1024]{3,2,1,0:T(8,128)(2,1)S(1)}, bf16[1,1,64,1024]{3,2,1,0:T(8,128)(2,1)S(1)}, u32[]{:S(2)}, u32[]{:S(2)}) collective-permute-start(bf16[1,1,64,1024]{3,2,1,0:T(8,128)(2,1)S(1)} %get-tuple-element.22), channel_id=1, source_target_pairs={{0,1},{1,2},{2,3},{3,4},{4,5},{5,6},{6,7},{8,9},{9,10},{10,11},{11... | collective-permute-start | bytes 393224 | tf_op jit(solution)/shard_map/ppermute | solution.py:15
  53.8 1.3 copy-start.5
  55.1 8.4 %copy-start = (bf16[1,16,576,1024]{3,2,1,0:T(8,128)(2,1)}, bf16[1,16,576,1024]{3,2,1,0:T(8,128)(2,1)S(1)}, u32[]{:S(2)}) copy-start(bf16[1,16,576,1024]{3,2,1,0:T(8,128)(2,1)S(1)} %fusion.69) | copy-start | bytes 56623108
  76.0 6.0 %collective-permute-start.5 = (bf16[1,1,64,1024]{3,2,1,0:T(8,128)(2,1)S(1)}, bf16[1,1,64,1024]{3,2,1,0:T(8,128)(2,1)S(1)}, u32[]{:S(2)}, u32[]{:S(2)}) collective-permute-start(bf16[1,1,64,1024]{3,2,1,0:T(8,128)(2,1)S(1)} %get-tuple-element.15), channel_id=1, source_target_pairs={{0,1},{1,2},{2,3},{3,4},{4,5},{5,6},{6,7},{8,9},{9,10},{10,11},{11... | collective-permute-start | bytes 393224 | tf_op jit(solution)/shard_map/ppermute | solution.py:15
  80.0 7.6 %collective-permute-start.4 = (bf16[1,1,64,1024]{3,2,1,0:T(8,128)(2,1)S(1)}, bf16[1,1,64,1024]{3,2,1,0:T(8,128)(2,1)S(1)}, u32[]{:S(2)}, u32[]{:S(2)}) collective-permute-start(bf16[1,1,64,1024]{3,2,1,0:T(8,128)(2,1)S(1)} %get-tuple-element.16), channel_id=1, source_target_pairs={{1,0},{2,1},{3,2},{4,3},{5,4},{6,5},{7,6},{9,8},{10,9},{11,10},{12... | collective-permute-start | bytes 393224 | tf_op jit(solution)/shard_map/ppermute | solution.py:16
  120.8 9.3 %collective-permute-start.7 = (bf16[1,1,64,1024]{3,2,1,0:T(8,128)(2,1)S(1)}, bf16[1,1,64,1024]{3,2,1,0:T(8,128)(2,1)S(1)}, u32[]{:S(2)}, u32[]{:S(2)}) collective-permute-start(bf16[1,1,64,1024]{3,2,1,0:T(8,128)(2,1)S(1)} %get-tuple-element.9), channel_id=1, source_target_pairs={{0,1},{1,2},{2,3},{3,4},{4,5},{5,6},{6,7},{8,9},{9,10},{10,11},{11... | collective-permute-start | bytes 393224 | tf_op jit(solution)/shard_map/ppermute | solution.py:15
  128.2 9.7 %collective-permute-start.6 = (bf16[1,1,64,1024]{3,2,1,0:T(8,128)(2,1)S(1)}, bf16[1,1,64,1024]{3,2,1,0:T(8,128)(2,1)S(1)}, u32[]{:S(2)}, u32[]{:S(2)}) collective-permute-start(bf16[1,1,64,1024]{3,2,1,0:T(8,128)(2,1)S(1)} %get-tuple-element.10), channel_id=1, source_target_pairs={{1,0},{2,1},{3,2},{4,3},{5,4},{6,5},{7,6},{9,8},{10,9},{11,10},{12... | collective-permute-start | bytes 393224 | tf_op jit(solution)/shard_map/ppermute | solution.py:16
Sparse Core Ops, SparseCore 0:
  120.8 365.1 all-gather.3
